TPU v7x, 256 devices: a whole 4x4x8 slice. The times are simulated.
256 devices in a mesh: tm: 256 (over y, z, x, core).
Axes of the slice: x: 4, y: 4, z: 8, core: 2. Of those that a mesh axis runs over, the one named last changes fastest.
Arguments:
- step_ops: float32 [512, 256, 256], P('tm')
- sources: float32 [512, 256], P('tm'), may hold values from -0.3 to 0.3
- terminal: float32 [256], replicated, may hold values from -6 to 6
- inertia_jac: float32 [512, 64], P('tm')
- gen_bus: int32 [64], replicated, may hold values from 0 to 255, as said below
Outputs:
- adjoint_states: float32 [512, 256], P('tm')
- sensitivity: float32 [64], replicated
Inputs may be any that keep to these rules, and one draw needn't show every extreme that they name: `gen_bus`: the 64 entries are distinct state indices.
All inputs are finite; a program needn't handle non-finite values.
Results may differ from a plain program's by a relative error of at most 0.0003.
Values sent between devices are 32-bit elements; how exact they have to be, the bound alone decides.
No kernel may reach another device: no remote copies, remote signals or barrier semaphores. Data moves between devices by JAX's collectives and lax.ppermute only.
A program may use at most 256 MiB of HBM per device.

v0:
```python
import jax
import jax.numpy as jnp
from jax import lax
from jax.sharding import PartitionSpec as P


def prefix_2(value, axis, join, neutral):
    count, mine = (lax.axis_size(axis), lax.axis_index(axis))
    pieces = jax.tree.map(lambda part: lax.all_gather(part, axis), value)
    pieces = jax.tree.map(lambda part: part[::-1], pieces)
    mine = count - 1 - mine
    running = jax.tree.map(
        lambda part, zero: jnp.full_like(part, 0) + jnp.asarray(zero, part.dtype), value, neutral
    )

    def turn(position, running):
        longer = join(running, jax.tree.map(lambda part: part[position], pieces))
        return jax.tree.map(lambda new, old: jnp.where(position < mine, new, old), longer, running)

    return lax.fori_loop(0, count - 1, turn, running)


def matmul(left, right):
    return jnp.dot(left, right, precision=lax.Precision.HIGHEST, preferred_element_type=jnp.float32)


def combine(earlier, later):
    return (matmul(later[0], earlier[0]), matmul(later[0], earlier[1]) + later[1])


def on_device(step_ops, sources, terminal, inertia_jac, gen_bus):
    steps_here = step_ops.shape[0]
    width = step_ops.shape[1]
    block_map = step_ops[steps_here - 1]
    block_vec = sources[steps_here - 1]
    time_increment = 0
    block_map = matmul(step_ops[time_increment], block_map)
    block_vec = matmul(step_ops[time_increment], block_vec) + sources[time_increment]
    identity = (jnp.eye(width, dtype=jnp.float32), jnp.zeros((width,), jnp.float32))
    prefix = prefix_2((block_map, block_vec), "tm", combine, identity)
    lam_end = matmul(prefix[0], terminal) + prefix[1]
    states = []
    lam = lam_end
    for time_increment in range(steps_here - 1, -1, -1):
        lam = matmul(step_ops[time_increment], lam) + sources[time_increment]
        states.append(lam)
    adjoint_states = jnp.stack(states[::-1], axis=0)
    columns = lax.broadcasted_iota(jnp.int32, (gen_bus.shape[0], width), 1)
    selector = (columns == gen_bus[:, None]).astype(jnp.float32)
    picked = matmul(adjoint_states, selector.T)
    share = jnp.sum(picked * inertia_jac, axis=0)
    total = lax.psum(share, "tm")
    total_steps = steps_here * lax.axis_size("tm")
    sensitivity = total * float(total_steps) ** (-0.5)
    return (adjoint_states, sensitivity)


def solution(mesh):
    in_specs = (P("tm", None, None), P("tm", None), P(), P("tm", None), P())
    out_specs = (P("tm", None), P())
    return jax.shard_map(
        on_device, mesh=mesh, in_specs=in_specs, out_specs=out_specs, check_vma=False
    )
```

profile of v0, /device:TPU:1, one launch (start us, length us, event | category | flops | bytes accessed | tf_op | source)
XLA Modules:
  0.0 1046.5 jit_solution(16165328054481829497)
XLA Ops:
  7.2 2.1 fusion.10
  11.4 67.2 %all-gather.2 = f32[256,1,256]{2,1,0:T(1,128)S(1)} all-gather(f32[1,1,256]{2,1,0:T(1,128)S(1)} %bitcast.72), channel_id=3, replica_groups=mesh['tm'=256] {'tm'}, dimensions={0}, use_global_device_ids=true | all-gather | bytes 263168 | tf_op jit(solution)/shard_map/all_gather | solution.py:9
  78.8 149.0 %all-gather.5.cloned.1.call-done = f32[65536,256]{1,0:T(8,128)} async-done(((f32[256,256]{1,0:T(8,128)}), f32[65536,256]{1,0:T(8,128)}) %all-gather.5.cloned.1.call-update) | async-done | bytes 67108880 | tf_op jit(solution)/shard_map/all_gather | solution.py:9
  227.8 44.2 %rev.6 = f32[256,256,256]{2,1,0:T(8,128)} reverse(f32[256,256,256]{2,1,0:T(8,128)} %bitcast.2), dimensions={0} | reverse | bytes 134217728 | tf_op jit(solution)/shard_map/rev | solution.py:10
  272.0 691.4 %while.16 = (s32[]{:T(128)}, f32[256,256]{1,0:T(8,128)S(1)}, f32[256]{0:T(256)S(1)}, s32[]{:T(128)}, f32[256,256,256]{2,1,0:T(8,128)}, /*index=5*/f32[256,256]{1,0:T(8,128)S(1)}, s32[]{:T(128)}, s32[]{:T(128)}) while((s32[]{:T(128)}, f32[256,256]{1,0:T(8,128)S(1)}, f32[256]{0:T(256)S(1)}, s32[]{:T(128)}, ...), condition=%wide.region_1.2_spmd.clone, body=%wide.region_0.1_spmd.clone.sunk | while | flops 202179584 | bytes 1845375 | solution.py:20
  272.1 1.3 convolution_select_fusion.2
  293.8 1.3 convolution_select_fusion.2
  296.5 1.3 convolution_select_fusion.2
  299.2 1.3 convolution_select_fusion.2
  301.9 1.3 convolution_select_fusion.2
  304.6 1.3 convolution_select_fusion.2
  307.3 1.3 convolution_select_fusion.2
  345.3 1.3 convolution_select_fusion.2
  348.0 1.3 convolution_select_fusion.2
  350.7 1.3 convolution_select_fusion.2
  353.4 1.3 convolution_select_fusion.2
  356.1 1.3 convolution_select_fusion.2
  358.8 1.3 convolution_select_fusion.2
  396.8 1.3 convolution_select_fusion.2
  399.5 1.3 convolution_select_fusion.2
  402.2 1.3 convolution_select_fusion.2
  404.9 1.3 convolution_select_fusion.2
  407.6 1.3 convolution_select_fusion.2
  410.4 1.3 convolution_select_fusion.2
  448.3 1.3 convolution_select_fusion.2
  451.0 1.3 convolution_select_fusion.2
  453.7 1.3 convolution_select_fusion.2
  456.5 1.3 convolution_select_fusion.2
  459.2 1.3 convolution_select_fusion.2
  461.9 1.3 convolution_select_fusion.2
  499.8 1.3 convolution_select_fusion.2
  502.6 1.3 convolution_select_fusion.2
  505.3 1.3 convolution_select_fusion.2
  508.0 1.3 convolution_select_fusion.2
  510.7 1.3 convolution_select_fusion.2
  513.4 1.3 convolution_select_fusion.2
  551.4 1.3 convolution_select_fusion.2
  554.1 1.3 convolution_select_fusion.2
  556.8 1.3 convolution_select_fusion.2
  559.5 1.3 convolution_select_fusion.2
  562.2 1.3 convolution_select_fusion.2
  564.9 1.3 convolution_select_fusion.2
  602.9 1.3 convolution_select_fusion.2
  605.6 1.3 convolution_select_fusion.2
  608.3 1.3 convolution_select_fusion.2
  611.0 1.3 convolution_select_fusion.2
  613.7 1.3 convolution_select_fusion.2
  964.8 74.4 %psum.7 = f32[64]{0:T(128)S(1)} all-reduce(f32[64]{0:T(128)S(1)} %fusion.7), channel_id=1, replica_groups=mesh['tm'=256] {'tm'}, use_global_device_ids=true, to_apply=%region_3.4 | all-reduce | flops 64 | bytes 512 | tf_op jit(solution)/shard_map/psum | solution.py:52
  (1516 shorter events, 624.2 us)
Async XLA Ops:
  7.2 956.3 %copy-start = (f32[256]{0:T(256)S(1)}, f32[256]{0:T(256)}, u32[]{:S(2)}) copy-start(f32[256]{0:T(256)} %param.9) | copy-start | bytes 3076
  7.2 220.6 %all-gather.5.cloned.1.call-start = ((), (), s32[]{:S(2)}) async-start(), calls=%async_computation | async-start | bytes 67371008 | tf_op jit(solution)/shard_map/all_gather | solution.py:9
  227.8 736.0 %copy-start.1 = (f32[2,256,256]{2,1,0:T(8,128)S(1)}, f32[2,256,256]{2,1,0:T(8,128)}, u32[]{:S(2)}) copy-start(f32[2,256,256]{2,1,0:T(8,128)} %param.7) | copy-start | bytes 1572868
  227.8 736.7 %copy-start.3 = (f32[2,64]{1,0:T(2,128)S(1)}, f32[2,64]{1,0:T(2,128)}, u32[]{:S(2)}) copy-start(f32[2,64]{1,0:T(2,128)} %param.10) | copy-start | bytes 1540
  227.8 736.7 %copy-start.4 = (s32[64]{0:T(128)S(1)}, s32[64]{0:T(128)}, u32[]{:S(2)}) copy-start(s32[64]{0:T(128)} %param.11) | copy-start | bytes 772
  964.5 75.1 %copy-start.2 = (f32[2,256]{1,0:T(2,128)}, f32[2,256]{1,0:T(2,128)S(1)}, u32[]{:S(2)}) copy-start(f32[2,256]{1,0:T(2,128)S(1)} %pad_maximum_fusion) | copy-start | bytes 6148
Sparse Core Ops, SparseCore 0:
  11.6 216.1 all-gather.4
where the time goes:
time: 1060 us; the launch traced here: 1050 us
  matrix products  656 us (62%)
  waiting for transfers between devices  149 us (14%)
  blocking collectives  142 us (13%)
  local copies, waits for them, and re-layouts  65.5 us (6%)
  loops' own time  15.3 us (1%)
  between operations  14.2 us (1%)
    dot_general x516, matrix products, matmul(): jnp.dot(left, right, precision=lax.Precision.HIGHEST, preferred_element_t...  656 us
    all_gather x1, waiting for transfers between devices, prefix_2(): pieces = jax.tree.map(lambda part: lax.all_gather(part, axis), value)  149 us
    psum x1, blocking collectives, on_device(): total = lax.psum(share, 'tm')  74.4 us
    all_gather x1, blocking collectives, prefix_2(): pieces = jax.tree.map(lambda part: lax.all_gather(part, axis), value)  67.2 us
    rev x2, local copies, waits for them, and re-layouts, prefix_2(): pieces = jax.tree.map(lambda part: part[::-1], pieces)  44.4 us
  transfers between devices with their start and end apart: 1, of which 1 were waited for; matrix products, arithmetic and copies ran while one was open for 0% of the time, Pallas kernels for 0%

commit v1 on v0

--- a/solution.py
+++ b/solution.py
@@ -49,7 +49,7 @@
     selector = (columns == gen_bus[:, None]).astype(jnp.float32)
     picked = matmul(adjoint_states, selector.T)
     share = jnp.sum(picked * inertia_jac, axis=0)
-    total = lax.psum(share, "tm")
+    total = jnp.sum(lax.all_gather(share, "tm"), axis=0)
     total_steps = steps_here * lax.axis_size("tm")
     sensitivity = total * float(total_steps) ** (-0.5)
     return (adjoint_states, sensitivity)

time: 1060 us -> 1230 us (1.16)
  waiting for transfers between devices: 149 us -> 388 us
  blocking collectives: 142 us -> 67.1 us
    unnamed x1 -> x3, waiting for transfers between devices: 0.02 us -> 239 us
    psum x1 -> x0, blocking collectives: 74.4 us -> none  [on_device(): total = lax.psum(share, 'tm')]
  transfers between devices with their start and end apart: 1 -> 2, of which waited for: 1 -> 2; matrix products, arithmetic and copies ran while one was open for 0% -> 0% of each run, Pallas kernels for 0% -> 0%
where the time goes in v1:
time: 1230 us; the launch traced here: 1210 us
  matrix products  656 us (53%)
  waiting for transfers between devices  388 us (32%)
  local copies, waits for them, and re-layouts  67.3 us (5%)
  blocking collectives  67.1 us (5%)
  loops' own time  15.1 us (1%)
  between operations  14.2 us (1%)
    dot_general x516, matrix products, matmul(): jnp.dot(left, right, precision=lax.Precision.HIGHEST, preferred_element_t...  656 us
    unnamed x3, waiting for transfers between devices  239 us
    all_gather x1, waiting for transfers between devices, prefix_2(): pieces = jax.tree.map(lambda part: lax.all_gather(part, axis), value)  149 us
    all_gather x1, blocking collectives, prefix_2(): pieces = jax.tree.map(lambda part: lax.all_gather(part, axis), value)  67.1 us
    rev x2, local copies, waits for them, and re-layouts, prefix_2(): pieces = jax.tree.map(lambda part: part[::-1], pieces)  44.3 us
  transfers between devices with their start and end apart: 2, of which 2 were waited for; matrix products, arithmetic and copies ran while one was open for 0% of the time, Pallas kernels for 0%

profile of v1, /device:TPU:1, one launch (start us, length us, event | category | flops | bytes accessed | tf_op | source)
XLA Modules:
  0.0 1212.6 jit_solution(10227122875759349351)
XLA Ops:
  7.2 2.1 fusion.10
  11.5 67.1 %all-gather.3 = f32[256,1,256]{2,1,0:T(1,128)S(1)} all-gather(f32[1,1,256]{2,1,0:T(1,128)S(1)} %bitcast.72), channel_id=3, replica_groups=mesh['tm'=256] {'tm'}, dimensions={0}, use_global_device_ids=true | all-gather | bytes 263168 | tf_op jit(solution)/shard_map/all_gather | solution.py:9
  78.8 149.0 %all-gather.6.cloned.1.call-done = f32[65536,256]{1,0:T(8,128)} async-done(((f32[256,256]{1,0:T(8,128)}), f32[65536,256]{1,0:T(8,128)}) %all-gather.6.cloned.1.call-update) | async-done | bytes 67108880 | tf_op jit(solution)/shard_map/all_gather | solution.py:9
  227.8 44.2 %rev.6 = f32[256,256,256]{2,1,0:T(8,128)} reverse(f32[256,256,256]{2,1,0:T(8,128)} %bitcast.2), dimensions={0} | reverse | bytes 134217728 | tf_op jit(solution)/shard_map/rev | solution.py:10
  272.0 691.4 %while.16 = (s32[]{:T(128)}, f32[256,256]{1,0:T(8,128)S(1)}, f32[256]{0:T(256)S(1)}, s32[]{:T(128)}, f32[256,256,256]{2,1,0:T(8,128)}, /*index=5*/f32[256,256]{1,0:T(8,128)S(1)}, s32[]{:T(128)}, s32[]{:T(128)}) while((s32[]{:T(128)}, f32[256,256]{1,0:T(8,128)S(1)}, f32[256]{0:T(256)S(1)}, s32[]{:T(128)}, ...), condition=%wide.region_1.2_spmd.clone, body=%wide.region_0.1_spmd.clone.sunk | while | flops 202179584 | bytes 1845375 | solution.py:20
  272.1 1.3 convolution_select_fusion.2
  274.8 1.3 convolution_select_fusion.2
  285.6 1.3 convolution_select_fusion.2
  291.0 1.3 convolution_select_fusion.2
  296.5 1.3 convolution_select_fusion.2
  301.9 1.3 convolution_select_fusion.2
  307.3 1.3 convolution_select_fusion.2
  312.7 1.3 convolution_select_fusion.2
  318.2 1.3 convolution_select_fusion.2
  323.6 1.3 convolution_select_fusion.2
  329.0 1.3 convolution_select_fusion.2
  334.4 1.3 convolution_select_fusion.2
  339.9 1.3 convolution_select_fusion.2
  345.3 1.3 convolution_select_fusion.2
  350.7 1.3 convolution_select_fusion.2
  356.1 1.3 convolution_select_fusion.2
  361.5 1.3 convolution_select_fusion.2
  367.0 1.3 convolution_select_fusion.2
  372.4 1.3 convolution_select_fusion.2
  377.8 1.3 convolution_select_fusion.2
  388.7 1.3 convolution_select_fusion.2
  394.1 1.3 convolution_select_fusion.2
  399.5 1.3 convolution_select_fusion.2
  404.9 1.3 convolution_select_fusion.2
  410.4 1.3 convolution_select_fusion.2
  415.8 1.3 convolution_select_fusion.2
  421.2 1.3 convolution_select_fusion.2
  426.6 1.3 convolution_select_fusion.2
  432.0 1.3 convolution_select_fusion.2
  437.5 1.3 convolution_select_fusion.2
  442.9 1.3 convolution_select_fusion.2
  448.3 1.3 convolution_select_fusion.2
  453.7 1.3 convolution_select_fusion.2
  459.2 1.3 convolution_select_fusion.2
  464.6 1.3 convolution_select_fusion.2
  470.0 1.3 convolution_select_fusion.2
  475.4 1.3 convolution_select_fusion.2
  480.9 1.3 convolution_select_fusion.2
  491.7 1.3 convolution_select_fusion.2
  497.1 1.3 convolution_select_fusion.2
  502.5 1.3 convolution_select_fusion.2
  508.0 1.3 convolution_select_fusion.2
  965.7 238.5 %all-reduce.3.cloned.1.call-done = f32[16384]{0:T(1024)} async-done(((f32[16384]{0:T(1024)}), f32[16384]{0:T(1024)}) %all-reduce.3.cloned.1.call-update) | async-done | bytes 65552
  (1524 shorter events, 626.3 us)
Async XLA Ops:
  7.2 956.3 %copy-start = (f32[256]{0:T(256)S(1)}, f32[256]{0:T(256)}, u32[]{:S(2)}) copy-start(f32[256]{0:T(256)} %param.9) | copy-start | bytes 3076
  7.2 220.6 %all-gather.6.cloned.1.call-start = ((), (), s32[]{:S(2)}) async-start(), calls=%async_computation | async-start | bytes 67371008 | tf_op jit(solution)/shard_map/all_gather | solution.py:9
  9.4 1194.9 %all-reduce.3.cloned.1.call-start = ((), (), s32[]{:S(2)}) async-start(), calls=%async_computation.1 | async-start | bytes 131072
  227.8 736.0 %copy-start.1 = (f32[2,256,256]{2,1,0:T(8,128)S(1)}, f32[2,256,256]{2,1,0:T(8,128)}, u32[]{:S(2)}) copy-start(f32[2,256,256]{2,1,0:T(8,128)} %param.7) | copy-start | bytes 1572868
  227.8 736.7 %copy-start.4 = (f32[2,64]{1,0:T(2,128)S(1)}, f32[2,64]{1,0:T(2,128)}, u32[]{:S(2)}) copy-start(f32[2,64]{1,0:T(2,128)} %param.10) | copy-start | bytes 1540
  227.8 736.7 %copy-start.5 = (s32[64]{0:T(128)S(1)}, s32[64]{0:T(128)}, u32[]{:S(2)}) copy-start(s32[64]{0:T(128)} %param.11) | copy-start | bytes 772
  964.5 241.2 %copy-start.3 = (f32[2,256]{1,0:T(2,128)}, f32[2,256]{1,0:T(2,128)S(1)}, u32[]{:S(2)}) copy-start(f32[2,256]{1,0:T(2,128)S(1)} %pad_maximum_fusion) | copy-start | bytes 6148
  965.0 0.6 copy-start.2
Sparse Core Ops, SparseCore 0:
  11.6 216.1 all-gather.5
  965.8 238.3 all-reduce.2
